TPU v7x, 512 devices: a whole 4x4x16 slice. The times are simulated.
512 devices in a mesh: gx: 32 (over y, z_lo), gy: 16 (over x, z_hi, core).
Axes of the slice: x: 4, y: 4, z: 16 (z_hi: 2, z_lo: 8; z = z_hi * 8 + z_lo), core: 2. Of those that a mesh axis runs over, the one named last changes fastest.
Arguments:
- latent: bfloat16 [128, 2048, 128], P('gx', 'gy'), may hold values from -6 to 6
- corr_kernel: bfloat16 [128, 128], replicated, may hold values from -0.5 to 0.5
- first_conv_weight: bfloat16 [3, 3, 128, 128], replicated, may hold values from -0.1875 to 0.1875
- first_conv_bias: float32 [128], replicated, may hold values from -3 to 3
- second_conv_weight: bfloat16 [3, 3, 128, 128], replicated, may hold values from -0.1875 to 0.1875
- second_conv_bias: float32 [128], replicated, may hold values from -3 to 3
- cotangent: bfloat16 [128, 2048, 128], P('gx', 'gy'), may hold values from -0.01171875 to 0.01171875
Outputs:
- prediction: bfloat16 [128, 2048, 128], P('gx', 'gy')
- conv1_weight_grad: float32 [3, 3, 128, 128], replicated
- conv1_bias_grad: float32 [128], replicated
- conv2_weight_grad: float32 [3, 3, 128, 128], replicated
- conv2_bias_grad: float32 [128], replicated
- kernel_grad: float32 [128, 128], replicated
All inputs are finite; a program needn't handle non-finite values.
Results may differ from a plain program's by a relative error of at most 0.0095.
Values may be sent and summed in bfloat16 or wider, within the bound.
No kernel may reach another device: no remote copies, remote signals or barrier semaphores. Data moves between devices by JAX's collectives and lax.ppermute only.
A program may use at most 64 MiB of HBM per device.

v0:
```python
import math
import jax
import jax.numpy as jnp
from jax import lax
from jax.sharding import PartitionSpec as P

DILATION_FIRST = 1
DILATION_SECOND = 2


def padded_2(array, sides, width):
    for axis, dim in sides:
        size, length = (lax.axis_size(axis), array.shape[dim])
        up = [(i, (i + 1) % size) for i in range(size)]
        down = [(j, i) for i, j in up]
        last = lax.slice_in_dim(array, length - width, length, axis=dim)
        leading = lax.slice_in_dim(array, 0, width, axis=dim)
        before = lax.ppermute(last, axis, up)
        after = lax.ppermute(leading, axis, down)
        array = jnp.concatenate([before, array, after], axis=dim)
    return array


def silu_slope(preact):
    logistic = jax.nn.sigmoid(preact)
    return logistic * (1.0 + preact * (1.0 - logistic))


def spectral_tables(length):
    positions = jnp.arange(length, dtype=jnp.int32)
    phases = positions[:, None] * positions[None, :] % length
    angles = phases.astype(jnp.float32) * (2.0 * math.pi / length)
    return (jnp.cos(angles), jnp.sin(angles))


def transform(table_mat, operand):
    return jnp.dot(
        table_mat, operand, precision=lax.Precision.HIGHEST, preferred_element_type=jnp.float32
    )


def to_columns(field):
    return lax.all_to_all(field, "gx", split_axis=1, concat_axis=0, tiled=True)


def surround(field, dilation):
    return padded_2(field, (("gx", 0), ("gy", 1)), dilation)


def forward_taps(padded, dilation, row_count, col_count, channels):
    windows = []
    for row_off in (-1, 0, 1):
        for col_off in (-1, 0, 1):
            row_at = dilation + row_off * dilation
            col_at = dilation + col_off * dilation
            windows.append(padded[row_at : row_at + row_count, col_at : col_at + col_count])
    return jnp.concatenate(windows, axis=-1).reshape(-1, 9 * channels)


def backward_taps(padded, dilation, row_count, col_count, channels):
    windows = []
    for row_off in (-1, 0, 1):
        for col_off in (-1, 0, 1):
            row_at = dilation - row_off * dilation
            col_at = dilation - col_off * dilation
            windows.append(padded[row_at : row_at + row_count, col_at : col_at + col_count])
    return jnp.concatenate(windows, axis=-1).reshape(-1, 9 * channels)


def layer_back(stored_item, gradient, row_count, col_count, channels):
    stacked, preact, weight, dilation = stored_item
    slope = (gradient * silu_slope(preact)).astype(jnp.bfloat16)
    flat_slope = slope.reshape(-1, channels)
    weight_grad = lax.dot_general(
        stacked, flat_slope, (((0,), (0,)), ((), ())), preferred_element_type=jnp.float32
    ).reshape(3, 3, channels, channels)
    bias_grad = jnp.sum(flat_slope.astype(jnp.float32), axis=0)
    stacked_back = backward_taps(
        surround(slope, dilation), dilation, row_count, col_count, channels
    )
    flipped = jnp.transpose(weight, (0, 1, 3, 2)).reshape(9 * channels, channels)
    carried = gradient + jnp.dot(stacked_back, flipped, preferred_element_type=jnp.float32).reshape(
        gradient.shape
    )
    return (weight_grad, bias_grad, carried)


def per_device(
    latent,
    corr_kernel,
    first_conv_weight,
    first_conv_bias,
    second_conv_weight,
    second_conv_bias,
    cotangent,
):
    row_count, col_count, channels = latent.shape
    full_rows = row_count * lax.axis_size("gx")
    columns = to_columns(latent)
    col_shape = columns.shape
    cosines, sines = spectral_tables(full_rows)
    flattened = columns.reshape(full_rows, -1).astype(jnp.float32)
    lat_real = transform(cosines, flattened).reshape(col_shape)
    lat_imag = (-transform(sines, flattened)).reshape(col_shape)
    kernel_f = corr_kernel.astype(jnp.float32)
    ker_real = transform(cosines, kernel_f)[:, None, :]
    ker_imag = (-transform(sines, kernel_f))[:, None, :]
    prod_real = (lat_real * ker_real + lat_imag * ker_imag).reshape(full_rows, -1)
    prod_imag = (lat_imag * ker_real - lat_real * ker_imag).reshape(full_rows, -1)
    correlated = (transform(cosines, prod_real) - transform(sines, prod_imag)) / full_rows
    mixed_cols = (columns.astype(jnp.float32) + correlated.reshape(col_shape)).astype(jnp.bfloat16)
    mixed_field = lax.all_to_all(mixed_cols, "gx", split_axis=0, concat_axis=1, tiled=True)
    stored = []
    current = mixed_field
    for weight, bias_vec, dilation in (
        (first_conv_weight, first_conv_bias, DILATION_FIRST),
        (second_conv_weight, second_conv_bias, DILATION_SECOND),
    ):
        stacked = forward_taps(
            surround(current, dilation), dilation, row_count, col_count, channels
        )
        preact = (
            jnp.dot(
                stacked, weight.reshape(9 * channels, channels), preferred_element_type=jnp.float32
            )
            + bias_vec
        )
        preact = preact.reshape(current.shape)
        stored.append((stacked, preact, weight, dilation))
        current = (current.astype(jnp.float32) + jax.nn.silu(preact)).astype(jnp.bfloat16)
    gradient = cotangent.astype(jnp.float32)
    second_weight_matrix, bias_two, gradient = layer_back(
        stored[1], gradient, row_count, col_count, channels
    )
    first_weight_matrix, bias_one, gradient = layer_back(
        stored[0], gradient, row_count, col_count, channels
    )
    mixed_gradient = gradient.astype(jnp.bfloat16)
    grad_cols = to_columns(mixed_gradient).reshape(full_rows, -1).astype(jnp.float32)
    grad_real = transform(cosines, grad_cols).reshape(col_shape)
    grad_imag = (-transform(sines, grad_cols)).reshape(col_shape)
    cross_real = jnp.sum(grad_real * lat_real + grad_imag * lat_imag, axis=1)
    cross_imag = jnp.sum(grad_real * lat_imag - grad_imag * lat_real, axis=1)
    kernel_grad = (transform(cosines, cross_real) - transform(sines, cross_imag)) / full_rows
    second_weight_matrix, bias_two, first_weight_matrix, bias_one, kernel_grad = lax.psum(
        (second_weight_matrix, bias_two, first_weight_matrix, bias_one, kernel_grad), ("gx", "gy")
    )
    return (current, first_weight_matrix, bias_one, second_weight_matrix, bias_two, kernel_grad)


def solution(mesh):
    in_specs = (P("gx", "gy", None), P(), P(), P(), P(), P(), P("gx", "gy", None))
    out_specs = (P("gx", "gy", None), P(), P(), P(), P(), P())
    return jax.shard_map(
        per_device, mesh=mesh, in_specs=in_specs, out_specs=out_specs, check_vma=False
    )
```

profile of v0, /device:TPU:4, one launch (start us, length us, event | category | flops | bytes accessed | tf_op | source)
XLA Modules:
  0.0 714.2 jit_solution(14996200767274391868)
XLA Ops:
  7.2 1.7 copy.39
  8.8 15.5 %all-to-all-start = ((bf16[4,128,128]{2,0,1:T(4,128)(2,1)}), bf16[4,128,128]{2,0,1:T(4,128)(2,1)S(1)}, u32[]{:S(2)}, u32[]{:S(2)}) async-start(bf16[4,128,128]{2,0,1:T(4,128)(2,1)} %copy.39), calls=%async_computation | async-start | bytes 262144 | tf_op jit(solution)/shard_map/all_to_all | solution.py:43
  25.4 13.4 %all-to-all-done = bf16[4,128,128]{2,0,1:T(4,128)(2,1)S(1)} async-done(((bf16[4,128,128]{2,0,1:T(4,128)(2,1)}), bf16[4,128,128]{2,0,1:T(4,128)(2,1)S(1)}, u32[]{:S(2)}, u32[]{:S(2)}) %all-to-all-start) | async-done | bytes 131104 | tf_op jit(solution)/shard_map/all_to_all | solution.py:43
  39.6 1.2 multiply_subtract_fusion
  40.8 0.6 fusion.30
  41.5 0.6 fusion
  42.3 18.7 %all_to_all.48 = bf16[128,4,128]{2,1,0:T(4,128)(2,1)S(1)} all-to-all(bf16[128,4,128]{2,1,0:T(4,128)(2,1)S(1)} %fusion.4), channel_id=1, replica_groups=mesh['gx'=32,'gy'=16] {'gx'}, dimensions={0} | all-to-all | bytes 262144 | tf_op jit(solution)/shard_map/all_to_all | solution.py:112
  61.1 2.2 collective-permute-start
  63.2 12.4 %collective-permute-start.1 = (bf16[1,128,128]{2,1,0:T(8,128)(2,1)S(1)}, bf16[1,128,128]{2,1,0:T(8,128)(2,1)S(1)}, u32[]{:S(2)}, u32[]{:S(2)}) collective-permute-start(bf16[1,128,128]{2,1,0:T(8,128)(2,1)S(1)} %bitcast.165), channel_id=1, source_target_pairs={{16,0},{32,16},{48,32},{64,48},{80,64},{96,80},{112,96},{128,112},... | collective-permute-start | bytes 98312 | tf_op jit(solution)/shard_map/ppermute | solution.py:19
  75.7 1.6 collective-permute-done.1
  77.2 1.9 collective-permute-start.2
  79.2 13.3 %collective-permute-start.3 = (bf16[6,1,128]{2,1,0:T(2,128)(2,1)S(1)}, bf16[6,1,128]{2,1,0:T(2,128)(2,1)S(1)}, u32[]{:S(2)}, u32[]{:S(2)}) collective-permute-start(bf16[6,1,128]{2,1,0:T(2,128)(2,1)S(1)} %get-tuple-element.40), channel_id=1, source_target_pairs={{1,0},{2,1},{3,2},{4,3},{5,4},{6,5},{7,6},{8,7},{9,8},{10,9},{11,1... | collective-permute-start | bytes 4616 | tf_op jit(solution)/shard_map/ppermute | solution.py:19
  92.5 1.3 collective-permute-done.3
  94.3 0.6 copy-done.2
  95.5 1.9 collective-permute-start.4
  97.4 12.9 %collective-permute-start.5 = (bf16[2,128,128]{2,1,0:T(8,128)(2,1)S(1)}, bf16[2,128,128]{2,1,0:T(8,128)(2,1)S(1)}, u32[]{:S(2)}, u32[]{:S(2)}) collective-permute-start(bf16[2,128,128]{2,1,0:T(8,128)(2,1)S(1)} %get-tuple-element.47), channel_id=1, source_target_pairs={{16,0},{32,16},{48,32},{64,48},{80,64},{96,80},{112,96},{128,112},... | collective-permute-start | bytes 196616 | tf_op jit(solution)/shard_map/ppermute | solution.py:19
  110.7 1.6 collective-permute-done.5
  112.3 6.5 collective-permute-start.6
  118.8 8.6 %collective-permute-start.7 = (bf16[8,2,128]{2,1,0:T(2,128)(2,1)S(1)}, bf16[8,2,128]{2,1,0:T(2,128)(2,1)S(1)}, u32[]{:S(2)}, u32[]{:S(2)}) collective-permute-start(bf16[8,2,128]{2,1,0:T(2,128)(2,1)S(1)} %get-tuple-element.26), channel_id=1, source_target_pairs={{1,0},{2,1},{3,2},{4,3},{5,4},{6,5},{7,6},{8,7},{9,8},{10,9},{11,1... | collective-permute-start | bytes 12296 | tf_op jit(solution)/shard_map/ppermute | solution.py:19
  127.5 1.3 collective-permute-done.7
  129.9 1.3 convert_reduce_fusion
  131.2 1.9 collective-permute-start.8
  133.1 13.1 %collective-permute-start.9 = (bf16[2,128,128]{2,1,0:T(8,128)(2,1)S(1)}, bf16[2,128,128]{2,1,0:T(8,128)(2,1)S(1)}, u32[]{:S(2)}, u32[]{:S(2)}) collective-permute-start(bf16[2,128,128]{2,1,0:T(8,128)(2,1)S(1)} %get-tuple-element.45), channel_id=1, source_target_pairs={{16,0},{32,16},{48,32},{64,48},{80,64},{96,80},{112,96},{128,112},... | collective-permute-start | bytes 196616 | tf_op jit(solution)/shard_map/ppermute | solution.py:19
  146.5 1.6 collective-permute-done.9
  148.1 12.5 %collective-permute-start.10 = (bf16[8,2,128]{2,1,0:T(2,128)(2,1)S(1)}, bf16[8,2,128]{2,1,0:T(2,128)(2,1)S(1)}, u32[]{:S(2)}, u32[]{:S(2)}) collective-permute-start(bf16[8,2,128]{2,1,0:T(2,128)(2,1)S(1)} %get-tuple-element.22), channel_id=1, source_target_pairs={{1,0},{2,1},{3,2},{4,3},{5,4},{6,5},{7,6},{8,7},{9,8},{10,9},{11,1... | collective-permute-start | bytes 12296 | tf_op jit(solution)/shard_map/ppermute | solution.py:19
  160.6 1.9 collective-permute-start.11
  162.8 12.4 %collective-permute-done.11 = bf16[8,2,128]{2,1,0:T(2,128)(2,1)S(1)} collective-permute-done((bf16[8,2,128]{2,1,0:T(2,128)(2,1)S(1)}, bf16[8,2,128]{2,1,0:T(2,128)(2,1)S(1)}, u32[]{:S(2)}, u32[]{:S(2)}) %collective-permute-start.11) | collective-permute-done | bytes 4128 | tf_op jit(solution)/shard_map/ppermute | solution.py:18
  175.7 1.2 convert_reduce_fusion.1
  176.9 1.9 collective-permute-start.12
  178.8 12.7 %collective-permute-start.13 = (bf16[1,128,128]{2,1,0:T(8,128)(2,1)S(1)}, bf16[1,128,128]{2,1,0:T(8,128)(2,1)S(1)}, u32[]{:S(2)}, u32[]{:S(2)}) collective-permute-start(bf16[1,128,128]{2,1,0:T(8,128)(2,1)S(1)} %get-tuple-element.43), channel_id=1, source_target_pairs={{16,0},{32,16},{48,32},{64,48},{80,64},{96,80},{112,96},{128,112},... | collective-permute-start | bytes 98312 | tf_op jit(solution)/shard_map/ppermute | solution.py:19
  191.5 1.6 collective-permute-done.13
  193.1 1.9 collective-permute-start.14
  195.0 2.4 collective-permute-start.15
  197.7 0.6 copy.46
  198.3 1.6 copy.48
  199.9 9.7 %collective-permute-done.15 = bf16[6,1,128]{2,1,0:T(2,128)(2,1)S(1)} collective-permute-done((bf16[6,1,128]{2,1,0:T(2,128)(2,1)S(1)}, bf16[6,1,128]{2,1,0:T(2,128)(2,1)S(1)}, u32[]{:S(2)}, u32[]{:S(2)}) %collective-permute-start.15) | collective-permute-done | bytes 1568 | tf_op jit(solution)/shard_map/ppermute | solution.py:18
  211.1 0.8 copy.50
  211.8 12.7 %all-to-all-start.2 = ((bf16[4,128,128]{2,0,1:T(4,128)(2,1)}), bf16[4,128,128]{2,0,1:T(4,128)(2,1)S(1)}, u32[]{:S(2)}, u32[]{:S(2)}) async-start(bf16[4,128,128]{2,0,1:T(4,128)(2,1)} %copy.50), calls=%async_computation.2 | async-start | bytes 262144 | tf_op jit(solution)/shard_map/all_to_all | solution.py:43
  224.8 1.3 fusion.89
  226.0 1.3 fusion.88
  227.3 10.1 %all-to-all-done.2 = bf16[4,128,128]{2,0,1:T(4,128)(2,1)S(1)} async-done(((bf16[4,128,128]{2,0,1:T(4,128)(2,1)}), bf16[4,128,128]{2,0,1:T(4,128)(2,1)S(1)}, u32[]{:S(2)}, u32[]{:S(2)}) %all-to-all-start.2) | async-done | bytes 131104 | tf_op jit(solution)/shard_map/all_to_all | solution.py:43
  238.3 0.5 subtract_reduce_fusion
  239.3 1.1 fusion.2
  240.4 102.9 %all-reduce = (f32[128]{0:T(128)}, f32[128]{0:T(128)}) all-reduce(f32[128]{0:T(128)S(1)} %get-tuple-element.15, f32[128]{0:T(128)S(1)} %get-tuple-element.13), channel_id=1, replica_groups=mesh['gx'=32,'gy'=16] {'gx','gy'}, use_global_device_ids=true, to_apply=%region_2.3 | all-reduce | flops 256 | bytes 2048 | tf_op jit(solution)/shard_map/psum | solution.py:145
  343.4 360.6 %all-reduce.4.cloned.1.call-done = (f32[3,3,128,128]{3,2,1,0:T(8,128)}, f32[3,3,128,128]{3,2,1,0:T(8,128)}, f32[128,128]{1,0:T(8,128)}) async-done(((f32[3,3,128,128]{3,2,1,0:T(8,128)}, f32[3,3,128,128]{3,2,1,0:T(8,128)}, f32[128,128]{1,0:T(8,128)}), (f32[3,3,128,128]{3,2,1,0:T(8,128)}, f32[3,3,128,128]{3,2,1,0:T(8,128)}, f32[128,128]{1,0:T(8,128)})) %all-reduce.4.cloned.1.call-update) | async-done | bytes 1245200 | tf_op jit(solution)/shard_map/psum | solution.py:145
  704.0 2.0 copy.112
  705.9 0.8 copy.113
  706.8 0.6 copy.114
  (103 shorter events, 8.7 us)
Async XLA Ops:
  7.2 17.2 %copy-start = (bf16[128,128]{1,0:T(8,128)(2,1)S(1)}, bf16[128,128]{1,0:T(8,128)(2,1)}, u32[]{:S(2)}) copy-start(bf16[128,128]{1,0:T(8,128)(2,1)} %param.8) | copy-start | bytes 98308
  8.8 29.9 %all-to-all-start = ((bf16[4,128,128]{2,0,1:T(4,128)(2,1)}), bf16[4,128,128]{2,0,1:T(4,128)(2,1)S(1)}, u32[]{:S(2)}, u32[]{:S(2)}) async-start(bf16[4,128,128]{2,0,1:T(4,128)(2,1)} %copy.39), calls=%async_computation | async-start | bytes 262144 | tf_op jit(solution)/shard_map/all_to_all | solution.py:43
  61.1 14.6 %collective-permute-start = (bf16[1,128,128]{2,1,0:T(8,128)(2,1)S(1)}, bf16[1,128,128]{2,1,0:T(8,128)(2,1)S(1)}, u32[]{:S(2)}, u32[]{:S(2)}) collective-permute-start(bf16[1,128,128]{2,1,0:T(8,128)(2,1)S(1)} %bitcast.166), channel_id=1, source_target_pairs={{0,16},{16,32},{32,48},{48,64},{64,80},{80,96},{96,112},{112,128},... | collective-permute-start | bytes 98312 | tf_op jit(solution)/shard_map/ppermute | solution.py:18
  63.2 14.0 %collective-permute-start.1 = (bf16[1,128,128]{2,1,0:T(8,128)(2,1)S(1)}, bf16[1,128,128]{2,1,0:T(8,128)(2,1)S(1)}, u32[]{:S(2)}, u32[]{:S(2)}) collective-permute-start(bf16[1,128,128]{2,1,0:T(8,128)(2,1)S(1)} %bitcast.165), channel_id=1, source_target_pairs={{16,0},{32,16},{48,32},{64,48},{80,64},{96,80},{112,96},{128,112},... | collective-permute-start | bytes 98312 | tf_op jit(solution)/shard_map/ppermute | solution.py:19
  77.2 15.2 %collective-permute-start.2 = (bf16[6,1,128]{2,1,0:T(2,128)(2,1)S(1)}, bf16[6,1,128]{2,1,0:T(2,128)(2,1)S(1)}, u32[]{:S(2)}, u32[]{:S(2)}) collective-permute-start(bf16[6,1,128]{2,1,0:T(2,128)(2,1)S(1)} %get-tuple-element.41), channel_id=1, source_target_pairs={{0,1},{1,2},{2,3},{3,4},{4,5},{5,6},{6,7},{7,8},{8,9},{9,10},{10,1... | collective-permute-start | bytes 4616 | tf_op jit(solution)/shard_map/ppermute | solution.py:18
  79.2 14.6 %collective-permute-start.3 = (bf16[6,1,128]{2,1,0:T(2,128)(2,1)S(1)}, bf16[6,1,128]{2,1,0:T(2,128)(2,1)S(1)}, u32[]{:S(2)}, u32[]{:S(2)}) collective-permute-start(bf16[6,1,128]{2,1,0:T(2,128)(2,1)S(1)} %get-tuple-element.40), channel_id=1, source_target_pairs={{1,0},{2,1},{3,2},{4,3},{5,4},{6,5},{7,6},{8,7},{9,8},{10,9},{11,1... | collective-permute-start | bytes 4616 | tf_op jit(solution)/shard_map/ppermute | solution.py:19
  94.0 1.0 copy-start.2
  94.0 1.0 copy-start.8
  95.5 15.2 %collective-permute-start.4 = (bf16[2,128,128]{2,1,0:T(8,128)(2,1)S(1)}, bf16[2,128,128]{2,1,0:T(8,128)(2,1)S(1)}, u32[]{:S(2)}, u32[]{:S(2)}) collective-permute-start(bf16[2,128,128]{2,1,0:T(8,128)(2,1)S(1)} %get-tuple-element.46), channel_id=1, source_target_pairs={{0,16},{16,32},{32,48},{48,64},{64,80},{80,96},{96,112},{112,128},... | collective-permute-start | bytes 196616 | tf_op jit(solution)/shard_map/ppermute | solution.py:18
  97.4 14.8 %collective-permute-start.5 = (bf16[2,128,128]{2,1,0:T(8,128)(2,1)S(1)}, bf16[2,128,128]{2,1,0:T(8,128)(2,1)S(1)}, u32[]{:S(2)}, u32[]{:S(2)}) collective-permute-start(bf16[2,128,128]{2,1,0:T(8,128)(2,1)S(1)} %get-tuple-element.47), channel_id=1, source_target_pairs={{16,0},{32,16},{48,32},{64,48},{80,64},{96,80},{112,96},{128,112},... | collective-permute-start | bytes 196616 | tf_op jit(solution)/shard_map/ppermute | solution.py:19
  112.3 15.2 %collective-permute-start.6 = (bf16[8,2,128]{2,1,0:T(2,128)(2,1)S(1)}, bf16[8,2,128]{2,1,0:T(2,128)(2,1)S(1)}, u32[]{:S(2)}, u32[]{:S(2)}) collective-permute-start(bf16[8,2,128]{2,1,0:T(2,128)(2,1)S(1)} %get-tuple-element.27), channel_id=1, source_target_pairs={{0,1},{1,2},{2,3},{3,4},{4,5},{5,6},{6,7},{7,8},{8,9},{9,10},{10,1... | collective-permute-start | bytes 12296 | tf_op jit(solution)/shard_map/ppermute | solution.py:18
  118.8 9.9 %collective-permute-start.7 = (bf16[8,2,128]{2,1,0:T(2,128)(2,1)S(1)}, bf16[8,2,128]{2,1,0:T(2,128)(2,1)S(1)}, u32[]{:S(2)}, u32[]{:S(2)}) collective-permute-start(bf16[8,2,128]{2,1,0:T(2,128)(2,1)S(1)} %get-tuple-element.26), channel_id=1, source_target_pairs={{1,0},{2,1},{3,2},{4,3},{5,4},{6,5},{7,6},{8,7},{9,8},{10,9},{11,1... | collective-permute-start | bytes 12296 | tf_op jit(solution)/shard_map/ppermute | solution.py:19
  128.9 1.0 copy-start.5
  128.9 1.0 copy-start.9
  129.0 1.0 copy-start.10
  129.4 1.8 copy-start.1
  131.2 15.3 %collective-permute-start.8 = (bf16[2,128,128]{2,1,0:T(8,128)(2,1)S(1)}, bf16[2,128,128]{2,1,0:T(8,128)(2,1)S(1)}, u32[]{:S(2)}, u32[]{:S(2)}) collective-permute-start(bf16[2,128,128]{2,1,0:T(8,128)(2,1)S(1)} %get-tuple-element.44), channel_id=1, source_target_pairs={{0,16},{16,32},{32,48},{48,64},{64,80},{80,96},{96,112},{112,128},... | collective-permute-start | bytes 196616 | tf_op jit(solution)/shard_map/ppermute | solution.py:18
  133.1 15.0 %collective-permute-start.9 = (bf16[2,128,128]{2,1,0:T(8,128)(2,1)S(1)}, bf16[2,128,128]{2,1,0:T(8,128)(2,1)S(1)}, u32[]{:S(2)}, u32[]{:S(2)}) collective-permute-start(bf16[2,128,128]{2,1,0:T(8,128)(2,1)S(1)} %get-tuple-element.45), channel_id=1, source_target_pairs={{16,0},{32,16},{48,32},{64,48},{80,64},{96,80},{112,96},{128,112},... | collective-permute-start | bytes 196616 | tf_op jit(solution)/shard_map/ppermute | solution.py:19
  148.1 14.6 %collective-permute-start.10 = (bf16[8,2,128]{2,1,0:T(2,128)(2,1)S(1)}, bf16[8,2,128]{2,1,0:T(2,128)(2,1)S(1)}, u32[]{:S(2)}, u32[]{:S(2)}) collective-permute-start(bf16[8,2,128]{2,1,0:T(2,128)(2,1)S(1)} %get-tuple-element.22), channel_id=1, source_target_pairs={{1,0},{2,1},{3,2},{4,3},{5,4},{6,5},{7,6},{8,7},{9,8},{10,9},{11,1... | collective-permute-start | bytes 12296 | tf_op jit(solution)/shard_map/ppermute | solution.py:19
  160.6 14.5 %collective-permute-start.11 = (bf16[8,2,128]{2,1,0:T(2,128)(2,1)S(1)}, bf16[8,2,128]{2,1,0:T(2,128)(2,1)S(1)}, u32[]{:S(2)}, u32[]{:S(2)}) collective-permute-start(bf16[8,2,128]{2,1,0:T(2,128)(2,1)S(1)} %get-tuple-element.21), channel_id=1, source_target_pairs={{0,1},{1,2},{2,3},{3,4},{4,5},{5,6},{6,7},{7,8},{8,9},{9,10},{10,1... | collective-permute-start | bytes 12296 | tf_op jit(solution)/shard_map/ppermute | solution.py:18
  176.9 14.6 %collective-permute-start.12 = (bf16[1,128,128]{2,1,0:T(8,128)(2,1)S(1)}, bf16[1,128,128]{2,1,0:T(8,128)(2,1)S(1)}, u32[]{:S(2)}, u32[]{:S(2)}) collective-permute-start(bf16[1,128,128]{2,1,0:T(8,128)(2,1)S(1)} %get-tuple-element.42), channel_id=1, source_target_pairs={{0,16},{16,32},{32,48},{48,64},{64,80},{80,96},{96,112},{112,128},... | collective-permute-start | bytes 98312 | tf_op jit(solution)/shard_map/ppermute | solution.py:18
  178.8 14.3 %collective-permute-start.13 = (bf16[1,128,128]{2,1,0:T(8,128)(2,1)S(1)}, bf16[1,128,128]{2,1,0:T(8,128)(2,1)S(1)}, u32[]{:S(2)}, u32[]{:S(2)}) collective-permute-start(bf16[1,128,128]{2,1,0:T(8,128)(2,1)S(1)} %get-tuple-element.43), channel_id=1, source_target_pairs={{16,0},{32,16},{48,32},{64,48},{80,64},{96,80},{112,96},{128,112},... | collective-permute-start | bytes 98312 | tf_op jit(solution)/shard_map/ppermute | solution.py:19
  193.1 6.8 collective-permute-start.14
  195.0 14.5 %collective-permute-start.15 = (bf16[6,1,128]{2,1,0:T(2,128)(2,1)S(1)}, bf16[6,1,128]{2,1,0:T(2,128)(2,1)S(1)}, u32[]{:S(2)}, u32[]{:S(2)}) collective-permute-start(bf16[6,1,128]{2,1,0:T(2,128)(2,1)S(1)} %get-tuple-element.36), channel_id=1, source_target_pairs={{0,1},{1,2},{2,3},{3,4},{4,5},{5,6},{6,7},{7,8},{8,9},{9,10},{10,1... | collective-permute-start | bytes 4616 | tf_op jit(solution)/shard_map/ppermute | solution.py:18
  209.6 1.0 copy-start.6
  211.8 25.6 %all-to-all-start.2 = ((bf16[4,128,128]{2,0,1:T(4,128)(2,1)}), bf16[4,128,128]{2,0,1:T(4,128)(2,1)S(1)}, u32[]{:S(2)}, u32[]{:S(2)}) async-start(bf16[4,128,128]{2,0,1:T(4,128)(2,1)} %copy.50), calls=%async_computation.2 | async-start | bytes 262144 | tf_op jit(solution)/shard_map/all_to_all | solution.py:43
  224.5 479.4 %all-reduce.4.cloned.1.call-start = ((), (), s32[]{:S(2)}) async-start(), calls=%async_computation.3 | async-start | bytes 2490368 | tf_op jit(solution)/shard_map/psum | solution.py:145
  227.3 11.0 %copy-start.3 = (f32[128,4,128]{0,2,1:T(8,128)S(1)}, f32[128,4,128]{0,2,1:T(8,128)}, u32[]{:S(2)}) copy-start(f32[128,4,128]{0,2,1:T(8,128)} %get-tuple-element.54) | copy-start | bytes 786436
  703.9 2.0 copy-start.4
  704.0 2.8 copy-start.7
Sparse Core Ops, SparseCore 0:
  240.6 463.3 all-reduce.3
where the time goes:
time: 715 us; the launch traced here: 714 us
  waiting for transfers between devices  416 us (58%)
  starting transfers between devices  137 us (19%)
  blocking collectives  122 us (17%)
  between operations  14.8 us (2%)
  matrix products  12.5 us (2%)
  local copies, waits for them, and re-layouts  12.3 us (2%)
    psum x1, waiting for transfers between devices, per_device(): lax.psum((second_weight_matrix, bias_two, first_weight_matrix, bias_one,...  361 us
    psum x1, blocking collectives, per_device(): lax.psum((second_weight_matrix, bias_two, first_weight_matrix, bias_one,...  103 us
    ppermute x8, starting transfers between devices, padded_2(): after = lax.ppermute(leading, axis, down)  87.4 us
    all_to_all x2, starting transfers between devices, to_columns(): return lax.all_to_all(field, 'gx', split_axis=1, concat_axis=0, tiled=True)  28.2 us
    all_to_all x2, waiting for transfers between devices, to_columns(): return lax.all_to_all(field, 'gx', split_axis=1, concat_axis=0, tiled=True)  23.5 us
    ppermute x8, waiting for transfers between devices, padded_2(): before = lax.ppermute(last, axis, up)  22.7 us
    ppermute x8, starting transfers between devices, padded_2(): before = lax.ppermute(last, axis, up)  20.7 us
    all_to_all x1, blocking collectives, per_device(): lax.all_to_all(mixed_cols, 'gx', split_axis=0, concat_axis=1, tiled=True)  18.7 us
  transfers between devices with their start and end apart: 19, of which 13 were waited for; matrix products, arithmetic and copies ran while one was open for 1% of the time, Pallas kernels for 0%

commit v1 on v0

--- a/solution.py
+++ b/solution.py
@@ -143,7 +143,10 @@
     cross_imag = jnp.sum(grad_real * lat_imag - grad_imag * lat_real, axis=1)
     kernel_grad = (transform(cosines, cross_real) - transform(sines, cross_imag)) / full_rows
     second_weight_matrix, bias_two, first_weight_matrix, bias_one, kernel_grad = lax.psum(
-        (second_weight_matrix, bias_two, first_weight_matrix, bias_one, kernel_grad), ("gx", "gy")
+        lax.psum(
+            (second_weight_matrix, bias_two, first_weight_matrix, bias_one, kernel_grad), "gx"
+        ),
+        "gy",
     )
     return (current, first_weight_matrix, bias_one, second_weight_matrix, bias_two, kernel_grad)
 

time: 715 us -> 1010 us (1.41)
  the two profiles are of different devices: /device:TPU:4 before, /device:TPU:104 now
where the time goes in v1:
time: 1010 us
  waiting for transfers between devices  653 us (65%)
  blocking collectives  195 us (19%)
  starting transfers between devices  122 us (12%)
  between operations  14.8 us (1%)
  matrix products  12.5 us (1%)
  local copies, waits for them, and re-layouts  12.3 us (1%)
    psum x1, waiting for transfers between devices, per_device(): lax.psum((second_weight_matrix, bias_two, first_weight_matrix, bias_one,...  425 us
    psum x1, waiting for transfers between devices, per_device(): lax.psum(lax.psum((second_weight_matrix, bias_two, first_weight_matrix, b...  157 us
    psum x1, blocking collectives, per_device(): lax.psum((second_weight_matrix, bias_two, first_weight_matrix, bias_one,...  107 us
    psum x1, blocking collectives, per_device(): lax.psum(lax.psum((second_weight_matrix, bias_two, first_weight_matrix, b...  68.9 us
    ppermute x8, starting transfers between devices, padded_2(): after = lax.ppermute(leading, axis, down)  51.8 us
    all_to_all x2, starting transfers between devices, to_columns(): return lax.all_to_all(field, 'gx', split_axis=1, concat_axis=0, tiled=True)  44.5 us
    ppermute x8, waiting for transfers between devices, padded_2(): after = lax.ppermute(leading, axis, down)  30.7 us
    ppermute x8, starting transfers between devices, padded_2(): before = lax.ppermute(last, axis, up)  25.2 us
  transfers between devices with their start and end apart: 20, of which 13 were waited for; matrix products, arithmetic and copies ran while one was open for 1% of the time, Pallas kernels for 0%

profile of v1, /device:TPU:104, one launch (start us, length us, event | category | flops | bytes accessed | tf_op | source)
XLA Modules:
  0.0 1010.3 jit_solution(4099063201699947330)
XLA Ops:
  7.2 1.7 copy.39
  8.8 14.4 %all-to-all-start = ((bf16[4,128,128]{2,0,1:T(4,128)(2,1)}), bf16[4,128,128]{2,0,1:T(4,128)(2,1)S(1)}, u32[]{:S(2)}, u32[]{:S(2)}) async-start(bf16[4,128,128]{2,0,1:T(4,128)(2,1)} %copy.39), calls=%async_computation | async-start | bytes 262144 | tf_op jit(solution)/shard_map/all_to_all | solution.py:43
  24.3 9.4 all-to-all-done
  34.5 1.2 multiply_subtract_fusion
  35.7 0.6 fusion.30
  36.3 0.7 fusion
  37.2 18.4 %all_to_all.48 = bf16[128,4,128]{2,1,0:T(4,128)(2,1)S(1)} all-to-all(bf16[128,4,128]{2,1,0:T(4,128)(2,1)S(1)} %fusion.4), channel_id=1, replica_groups=mesh['gx'=32,'gy'=16] {'gx'}, dimensions={0} | all-to-all | bytes 262144 | tf_op jit(solution)/shard_map/all_to_all | solution.py:112
  55.7 2.8 collective-permute-start
  58.5 3.1 collective-permute-start.1
  61.6 3.9 collective-permute-done.1
  65.5 1.9 collective-permute-start.2
  67.4 14.5 %collective-permute-start.3 = (bf16[6,1,128]{2,1,0:T(2,128)(2,1)S(1)}, bf16[6,1,128]{2,1,0:T(2,128)(2,1)S(1)}, u32[]{:S(2)}, u32[]{:S(2)}) collective-permute-start(bf16[6,1,128]{2,1,0:T(2,128)(2,1)S(1)} %get-tuple-element.45), channel_id=1, source_target_pairs={{1,0},{2,1},{3,2},{4,3},{5,4},{6,5},{7,6},{8,7},{9,8},{10,9},{11,1... | collective-permute-start | bytes 4616 | tf_op jit(solution)/shard_map/ppermute | solution.py:19
  82.0 1.3 collective-permute-done.3
  85.0 1.9 collective-permute-start.4
  86.9 3.9 collective-permute-start.5
  91.1 3.1 collective-permute-done.5
  94.3 5.1 collective-permute-start.6
  99.4 11.3 %collective-permute-start.7 = (bf16[8,2,128]{2,1,0:T(2,128)(2,1)S(1)}, bf16[8,2,128]{2,1,0:T(2,128)(2,1)S(1)}, u32[]{:S(2)}, u32[]{:S(2)}) collective-permute-start(bf16[8,2,128]{2,1,0:T(2,128)(2,1)S(1)} %get-tuple-element.31), channel_id=1, source_target_pairs={{1,0},{2,1},{3,2},{4,3},{5,4},{6,5},{7,6},{8,7},{9,8},{10,9},{11,1... | collective-permute-start | bytes 12296 | tf_op jit(solution)/shard_map/ppermute | solution.py:19
  110.7 1.3 collective-permute-done.7
  113.1 1.3 convert_reduce_fusion
  114.4 4.8 collective-permute-start.8
  119.3 1.9 collective-permute-start.9
  121.2 11.8 %collective-permute-done.9 = bf16[2,128,128]{2,1,0:T(8,128)(2,1)S(1)} collective-permute-done((bf16[2,128,128]{2,1,0:T(8,128)(2,1)S(1)}, bf16[2,128,128]{2,1,0:T(8,128)(2,1)S(1)}, u32[]{:S(2)}, u32[]{:S(2)}) %collective-permute-start.9) | collective-permute-done | bytes 65568 | tf_op jit(solution)/shard_map/ppermute | solution.py:19
  133.0 13.2 %collective-permute-start.10 = (bf16[8,2,128]{2,1,0:T(2,128)(2,1)S(1)}, bf16[8,2,128]{2,1,0:T(2,128)(2,1)S(1)}, u32[]{:S(2)}, u32[]{:S(2)}) collective-permute-start(bf16[8,2,128]{2,1,0:T(2,128)(2,1)S(1)} %get-tuple-element.27), channel_id=1, source_target_pairs={{1,0},{2,1},{3,2},{4,3},{5,4},{6,5},{7,6},{8,7},{9,8},{10,9},{11,1... | collective-permute-start | bytes 12296 | tf_op jit(solution)/shard_map/ppermute | solution.py:19
  146.2 1.9 collective-permute-start.11
  148.4 13.6 %collective-permute-done.11 = bf16[8,2,128]{2,1,0:T(2,128)(2,1)S(1)} collective-permute-done((bf16[8,2,128]{2,1,0:T(2,128)(2,1)S(1)}, bf16[8,2,128]{2,1,0:T(2,128)(2,1)S(1)}, u32[]{:S(2)}, u32[]{:S(2)}) %collective-permute-start.11) | collective-permute-done | bytes 4128 | tf_op jit(solution)/shard_map/ppermute | solution.py:18
  162.5 1.2 convert_reduce_fusion.1
  163.7 4.4 collective-permute-start.12
  168.1 1.9 collective-permute-start.13
  170.1 9.2 collective-permute-done.13
  179.3 1.9 collective-permute-start.14
  181.2 2.4 collective-permute-start.15
  183.9 0.6 copy.46
  184.5 1.6 copy.48
  186.1 10.9 %collective-permute-done.15 = bf16[6,1,128]{2,1,0:T(2,128)(2,1)S(1)} collective-permute-done((bf16[6,1,128]{2,1,0:T(2,128)(2,1)S(1)}, bf16[6,1,128]{2,1,0:T(2,128)(2,1)S(1)}, u32[]{:S(2)}, u32[]{:S(2)}) %collective-permute-start.15) | collective-permute-done | bytes 1568 | tf_op jit(solution)/shard_map/ppermute | solution.py:18
  198.5 0.8 copy.50
  199.3 30.1 %all-to-all-start.2 = ((bf16[4,128,128]{2,0,1:T(4,128)(2,1)}), bf16[4,128,128]{2,0,1:T(4,128)(2,1)S(1)}, u32[]{:S(2)}, u32[]{:S(2)}) async-start(bf16[4,128,128]{2,0,1:T(4,128)(2,1)} %copy.50), calls=%async_computation.2 | async-start | bytes 262144 | tf_op jit(solution)/shard_map/all_to_all | solution.py:43
  229.6 1.3 fusion.89
  230.9 1.3 fusion.88
  232.2 6.5 all-to-all-done.2
  240.5 1.1 fusion.2
  241.7 424.8 %all-reduce.7.cloned.1.call-done = (f32[3,3,128,128]{3,2,1,0:T(8,128)}, f32[3,3,128,128]{3,2,1,0:T(8,128)}, f32[128,128]{1,0:T(8,128)}) async-done(((f32[3,3,128,128]{3,2,1,0:T(8,128)}, f32[3,3,128,128]{3,2,1,0:T(8,128)}, f32[128,128]{1,0:T(8,128)}), (f32[3,3,128,128]{3,2,1,0:T(8,128)}, f32[3,3,128,128]{3,2,1,0:T(8,128)}, f32[128,128]{1,0:T(8,128)})) %all-reduce.7.cloned.1.call-update) | async-done | bytes 1245200 | tf_op jit(solution)/shard_map/psum | solution.py:146
  666.5 107.5 %all-reduce = (f32[128]{0:T(128)S(1)}, f32[128]{0:T(128)S(1)}) all-reduce(f32[128]{0:T(128)S(1)} %get-tuple-element.20, f32[128]{0:T(128)S(1)} %get-tuple-element.18), channel_id=1, replica_groups=mesh['gx'=32,'gy'=16] {'gx'}, use_global_device_ids=true, to_apply=%region_3.4 | all-reduce | flops 256 | bytes 2048 | tf_op jit(solution)/shard_map/psum | solution.py:146
  774.0 68.9 %all-reduce.2 = (f32[128]{0:T(128)}, f32[128]{0:T(128)}) all-reduce(f32[128]{0:T(128)S(1)} %get-tuple-element.8, f32[128]{0:T(128)S(1)} %get-tuple-element.9), channel_id=1, replica_groups=mesh['gx'=32,'gy'=16] {'gy'}, use_global_device_ids=true, to_apply=%region_4.5 | all-reduce | flops 256 | bytes 2048 | tf_op jit(solution)/shard_map/psum | solution.py:145
  842.9 157.2 %all-reduce.9.cloned.1.call-done = (f32[3,3,128,128]{3,2,1,0:T(8,128)}, f32[3,3,128,128]{3,2,1,0:T(8,128)}, f32[128,128]{1,0:T(8,128)}) async-done(((f32[3,3,128,128]{3,2,1,0:T(8,128)}, f32[3,3,128,128]{3,2,1,0:T(8,128)}, f32[128,128]{1,0:T(8,128)}), (f32[3,3,128,128]{3,2,1,0:T(8,128)}, f32[3,3,128,128]{3,2,1,0:T(8,128)}, f32[128,128]{1,0:T(8,128)})) %all-reduce.9.cloned.1.call-update) | async-done | bytes 1245200 | tf_op jit(solution)/shard_map/psum | solution.py:145
  1000.0 2.0 copy.115
  1002.0 0.8 copy.116
  1002.8 0.6 copy.117
  (107 shorter events, 9.6 us)
Async XLA Ops:
  7.2 16.1 %copy-start = (bf16[128,128]{1,0:T(8,128)(2,1)S(1)}, bf16[128,128]{1,0:T(8,128)(2,1)}, u32[]{:S(2)}) copy-start(bf16[128,128]{1,0:T(8,128)(2,1)} %param.8) | copy-start | bytes 98308
  8.8 24.8 %all-to-all-start = ((bf16[4,128,128]{2,0,1:T(4,128)(2,1)}), bf16[4,128,128]{2,0,1:T(4,128)(2,1)S(1)}, u32[]{:S(2)}, u32[]{:S(2)}) async-start(bf16[4,128,128]{2,0,1:T(4,128)(2,1)} %copy.39), calls=%async_computation | async-start | bytes 262144 | tf_op jit(solution)/shard_map/all_to_all | solution.py:43
  55.7 5.9 collective-permute-start
  58.5 7.0 collective-permute-start.1
  65.5 16.4 %collective-permute-start.2 = (bf16[6,1,128]{2,1,0:T(2,128)(2,1)S(1)}, bf16[6,1,128]{2,1,0:T(2,128)(2,1)S(1)}, u32[]{:S(2)}, u32[]{:S(2)}) collective-permute-start(bf16[6,1,128]{2,1,0:T(2,128)(2,1)S(1)} %get-tuple-element.46), channel_id=1, source_target_pairs={{0,1},{1,2},{2,3},{3,4},{4,5},{5,6},{6,7},{7,8},{8,9},{9,10},{10,1... | collective-permute-start | bytes 4616 | tf_op jit(solution)/shard_map/ppermute | solution.py:18
  67.4 15.8 %collective-permute-start.3 = (bf16[6,1,128]{2,1,0:T(2,128)(2,1)S(1)}, bf16[6,1,128]{2,1,0:T(2,128)(2,1)S(1)}, u32[]{:S(2)}, u32[]{:S(2)}) collective-permute-start(bf16[6,1,128]{2,1,0:T(2,128)(2,1)S(1)} %get-tuple-element.45), channel_id=1, source_target_pairs={{1,0},{2,1},{3,2},{4,3},{5,4},{6,5},{7,6},{8,7},{9,8},{10,9},{11,1... | collective-permute-start | bytes 4616 | tf_op jit(solution)/shard_map/ppermute | solution.py:19
  83.4 1.0 copy-start.2
  83.4 1.0 copy-start.8
  85.0 6.2 collective-permute-start.4
  86.9 7.4 collective-permute-start.5
  94.3 16.4 %collective-permute-start.6 = (bf16[8,2,128]{2,1,0:T(2,128)(2,1)S(1)}, bf16[8,2,128]{2,1,0:T(2,128)(2,1)S(1)}, u32[]{:S(2)}, u32[]{:S(2)}) collective-permute-start(bf16[8,2,128]{2,1,0:T(2,128)(2,1)S(1)} %get-tuple-element.32), channel_id=1, source_target_pairs={{0,1},{1,2},{2,3},{3,4},{4,5},{5,6},{6,7},{7,8},{8,9},{9,10},{10,1... | collective-permute-start | bytes 12296 | tf_op jit(solution)/shard_map/ppermute | solution.py:18
  99.4 12.6 %collective-permute-start.7 = (bf16[8,2,128]{2,1,0:T(2,128)(2,1)S(1)}, bf16[8,2,128]{2,1,0:T(2,128)(2,1)S(1)}, u32[]{:S(2)}, u32[]{:S(2)}) collective-permute-start(bf16[8,2,128]{2,1,0:T(2,128)(2,1)S(1)} %get-tuple-element.31), channel_id=1, source_target_pairs={{1,0},{2,1},{3,2},{4,3},{5,4},{6,5},{7,6},{8,7},{9,8},{10,9},{11,1... | collective-permute-start | bytes 12296 | tf_op jit(solution)/shard_map/ppermute | solution.py:19
  112.1 1.0 copy-start.5
  112.2 1.0 copy-start.9
  112.2 1.0 copy-start.10
  112.6 1.8 copy-start.1
  114.4 6.8 collective-permute-start.8
  119.3 13.7 %collective-permute-start.9 = (bf16[2,128,128]{2,1,0:T(8,128)(2,1)S(1)}, bf16[2,128,128]{2,1,0:T(8,128)(2,1)S(1)}, u32[]{:S(2)}, u32[]{:S(2)}) collective-permute-start(bf16[2,128,128]{2,1,0:T(8,128)(2,1)S(1)} %get-tuple-element.50), channel_id=1, source_target_pairs={{16,0},{32,16},{48,32},{64,48},{80,64},{96,80},{112,96},{128,112},... | collective-permute-start | bytes 196616 | tf_op jit(solution)/shard_map/ppermute | solution.py:19
  133.0 15.4 %collective-permute-start.10 = (bf16[8,2,128]{2,1,0:T(2,128)(2,1)S(1)}, bf16[8,2,128]{2,1,0:T(2,128)(2,1)S(1)}, u32[]{:S(2)}, u32[]{:S(2)}) collective-permute-start(bf16[8,2,128]{2,1,0:T(2,128)(2,1)S(1)} %get-tuple-element.27), channel_id=1, source_target_pairs={{1,0},{2,1},{3,2},{4,3},{5,4},{6,5},{7,6},{8,7},{9,8},{10,9},{11,1... | collective-permute-start | bytes 12296 | tf_op jit(solution)/shard_map/ppermute | solution.py:19
  146.2 15.7 %collective-permute-start.11 = (bf16[8,2,128]{2,1,0:T(2,128)(2,1)S(1)}, bf16[8,2,128]{2,1,0:T(2,128)(2,1)S(1)}, u32[]{:S(2)}, u32[]{:S(2)}) collective-permute-start(bf16[8,2,128]{2,1,0:T(2,128)(2,1)S(1)} %get-tuple-element.26), channel_id=1, source_target_pairs={{0,1},{1,2},{2,3},{3,4},{4,5},{5,6},{6,7},{7,8},{8,9},{9,10},{10,1... | collective-permute-start | bytes 12296 | tf_op jit(solution)/shard_map/ppermute | solution.py:18
  163.7 6.3 collective-permute-start.12
  168.1 11.2 %collective-permute-start.13 = (bf16[1,128,128]{2,1,0:T(8,128)(2,1)S(1)}, bf16[1,128,128]{2,1,0:T(8,128)(2,1)S(1)}, u32[]{:S(2)}, u32[]{:S(2)}) collective-permute-start(bf16[1,128,128]{2,1,0:T(8,128)(2,1)S(1)} %get-tuple-element.48), channel_id=1, source_target_pairs={{16,0},{32,16},{48,32},{64,48},{80,64},{96,80},{112,96},{128,112},... | collective-permute-start | bytes 98312 | tf_op jit(solution)/shard_map/ppermute | solution.py:19
  179.3 6.8 collective-permute-start.14
  181.2 15.7 %collective-permute-start.15 = (bf16[6,1,128]{2,1,0:T(2,128)(2,1)S(1)}, bf16[6,1,128]{2,1,0:T(2,128)(2,1)S(1)}, u32[]{:S(2)}, u32[]{:S(2)}) collective-permute-start(bf16[6,1,128]{2,1,0:T(2,128)(2,1)S(1)} %get-tuple-element.41), channel_id=1, source_target_pairs={{0,1},{1,2},{2,3},{3,4},{4,5},{5,6},{6,7},{7,8},{8,9},{9,10},{10,1... | collective-permute-start | bytes 4616 | tf_op jit(solution)/shard_map/ppermute | solution.py:18
  197.1 1.0 copy-start.6
  199.3 39.4 %all-to-all-start.2 = ((bf16[4,128,128]{2,0,1:T(4,128)(2,1)}), bf16[4,128,128]{2,0,1:T(4,128)(2,1)S(1)}, u32[]{:S(2)}, u32[]{:S(2)}) async-start(bf16[4,128,128]{2,0,1:T(4,128)(2,1)} %copy.50), calls=%async_computation.2 | async-start | bytes 262144 | tf_op jit(solution)/shard_map/all_to_all | solution.py:43
  229.4 437.1 %all-reduce.7.cloned.1.call-start = ((), (), s32[]{:S(2)}) async-start(), calls=%async_computation.3 | async-start | bytes 2490368 | tf_op jit(solution)/shard_map/psum | solution.py:146
  232.2 7.3 copy-start.3
  241.6 758.4 %all-reduce.9.cloned.1.call-start = ((), (), s32[]{:S(2)}) async-start(), calls=%async_computation.4 | async-start | bytes 2490368 | tf_op jit(solution)/shard_map/psum | solution.py:145
  1000.0 2.0 copy-start.4
  1000.0 2.8 copy-start.7
Sparse Core Ops, SparseCore 0:
  241.7 424.6 all-reduce.6
  669.9 330.0 all-reduce.8
